TPU v7x, 128 devices: a whole 4x4x4 slice. The times are simulated.
128 devices in a mesh: ctx: 32 (over y, z, core), exp: 4 (over x).
Axes of the slice: x: 4, y: 4, z: 4, core: 2. Of those that a mesh axis runs over, the one named last changes fastest.
Arguments:
- inputs: bfloat16 [4096, 4096], P('ctx', 'exp'), may hold values from -6 to 6
- gate_input: bfloat16 [4096, 4096], P('ctx', 'exp')
- b_proj: bfloat16 [4096, 128], P('ctx'), may hold values from -0.5 to 0.5
- c_proj: bfloat16 [4096, 128], P('ctx'), may hold values from -6 to 6
- step_size: float32 [64, 4096], P('exp', 'ctx'), may hold values from 0.03 to 0.3
- decay_rate: float32 [64, 4096], P('exp', 'ctx'), as said below
- skip_gain: float32 [64], P('exp'), may hold values from 0.5 to 2
- start_state: float32 [64, 64, 128], P('exp'), may hold values from -3 to 3
- norm_gain: float32 [4096], P('exp'), may hold values from 0.5 to 1.5
- out_proj: bfloat16 [4096, 4096], P('exp', 'ctx'), may hold values from -0.09375 to 0.09375
- residual: bfloat16 [4096, 4096], P('ctx'), may hold values from -6 to 6
- moe_gain: float32 [4096], replicated, may hold values from 0.5 to 1.5
- w_gate: bfloat16 [32, 4096, 3584], P('ctx', None, 'exp'), may hold values from -0.09375 to 0.09375
- w_up: bfloat16 [32, 4096, 3584], P('ctx', None, 'exp'), may hold values from -0.09375 to 0.09375
- w_down: bfloat16 [32, 3584, 4096], P('ctx', 'exp'), may hold values from -0.0625 to 0.0625
- route_ids: int32 [4096, 2], P('ctx'), may hold values from 0 to 15, all different within a row; in each aligned block of 32 rows (0 to 31, 32 to 63, ...) at most 8 rows name the same one
- route_gates: float32 [4096, 2], P('ctx'), may hold values from 0.3 to 1
Outputs:
- output: bfloat16 [4096, 4096], P(('ctx', 'exp'))
Inputs may be any that keep to these rules, and one draw needn't show every extreme that they name: `route_ids`: each row names two different experts. In each aligned block of 32 rows no expert is named more than 8 times, a bound that some block reaches. `decay_rate`: Non-negative.
All inputs are finite; a program needn't handle non-finite values.
Results may differ from a plain program's by a relative error of at most 0.02.
Values may be sent and summed in bfloat16 or wider, within the bound.
A program may use at most 128 MiB of HBM per device.

v0:
```python
import jax
import jax.numpy as jnp
from jax import lax
from jax.sharding import PartitionSpec as P

PAIR = 2
eps_norm = 1e-05
top_precision = lax.Precision.HIGHEST


def entering(x, axis, join, neutral):
    place = lax.axis_index(axis)
    decay, state = x
    packed = jnp.concatenate(
        [state, jnp.broadcast_to(decay[:, None, None], (state.shape[0], 1, state.shape[2]))], axis=1
    )
    gathered = lax.all_gather(packed.astype(jnp.bfloat16), axis)
    start = jax.tree.map(lambda a, e: jnp.zeros_like(a) + jnp.asarray(e, a.dtype), x, neutral)

    def one(hop, carry):
        block = lax.dynamic_index_in_dim(gathered, hop, 0, False).astype(jnp.float32)
        return join(carry, (block[:, -1, 0], block[:, :-1, :]))

    return lax.fori_loop(0, place, one, start)


def later_state(earlier, later):
    first_decay, first_state = earlier
    second_decay, second_state = later
    return (first_decay * second_decay, second_decay[:, None, None] * first_state + second_state)


def route_ranks(quarter_ids, experts):
    flattened = quarter_ids.reshape(-1)
    onehot = (flattened[:, None] == jnp.arange(experts, dtype=jnp.int32)[None, :]).astype(jnp.int32)
    running = jnp.cumsum(onehot, axis=0)
    rank_ids = jnp.sum(onehot * running, axis=1) - 1
    return (flattened, rank_ids)


def place_rows(normed, quarter_ids, experts, capacity):
    flattened, rank_ids = route_ranks(quarter_ids, experts)
    slot_ids = rank_ids * experts + flattened
    matches = (
        jnp.arange(capacity * experts, dtype=jnp.int32)[:, None] == slot_ids[None, :]
    ).astype(jnp.bfloat16)
    doubled = jnp.repeat(normed, quarter_ids.shape[1], axis=0)
    placed = jnp.dot(matches, doubled, preferred_element_type=jnp.float32).astype(jnp.bfloat16)
    return placed.reshape(capacity, experts, normed.shape[1])


def rms_rows(values, gain_vec):
    scaling = lax.rsqrt(jnp.mean(values * values, axis=1, keepdims=True) + eps_norm)
    return (values * scaling * gain_vec[None, :]).astype(jnp.bfloat16)


def local(
    inputs,
    gate_input,
    b_proj,
    c_proj,
    step_size,
    decay_rate,
    skip_gain,
    start_state,
    norm_gain,
    out_proj,
    residual,
    moe_gain,
    w_gate,
    w_up,
    w_down,
    route_ids,
    route_gates,
):
    tok_ctx = inputs.shape[0]
    head_count = step_size.shape[0]
    head_dim = inputs.shape[1] // head_count
    model_width = residual.shape[1]
    n_ctx = lax.axis_size("ctx")
    n_exp = lax.axis_size("exp")
    experts = n_ctx // PAIR
    tok_quarter = tok_ctx // n_exp
    capacity = 4 * tok_quarter // experts
    x_local = inputs.astype(jnp.float32).reshape(tok_ctx, head_count, head_dim)
    b_local = b_proj.astype(jnp.float32)
    c_local = c_proj.astype(jnp.float32)
    cumulative = jnp.cumsum(decay_rate, axis=1)
    span_total = cumulative[:, -1]
    sequence_indices = jnp.arange(tok_ctx, dtype=jnp.int32)
    causal = sequence_indices[:, None] >= sequence_indices[None, :]
    spread = jnp.where(causal[None], cumulative[:, :, None] - cumulative[:, None, :], 0.0)
    scores = jnp.dot(c_local, b_local.T, precision=top_precision)
    mixing = jnp.where(causal[None], jnp.exp(-spread), 0.0) * scores[None] * step_size[:, None, :]
    inside_part = jnp.einsum("hts,shp->thp", mixing, x_local, precision=top_precision)
    ending = jnp.exp(-(span_total[:, None] - cumulative)) * step_size
    local_state = jnp.einsum("hs,shp,sn->hpn", ending, x_local, b_local, precision=top_precision)
    prior_decay, prior_state = entering(
        (jnp.exp(-span_total), local_state),
        "ctx",
        later_state,
        (jnp.ones_like(span_total), jnp.zeros_like(local_state)),
    )
    incoming = prior_state + prior_decay[:, None, None] * start_state
    carried = (
        jnp.einsum("hpn,tn->thp", incoming, c_local, precision=top_precision)
        * jnp.exp(-cumulative).T[:, :, None]
    )
    ssm_out = inside_part + carried + skip_gain[None, :, None] * x_local
    gated_out = ssm_out.reshape(tok_ctx, head_count * head_dim) * jax.nn.silu(
        gate_input.astype(jnp.float32)
    )
    squares = lax.psum(jnp.sum(gated_out * gated_out, axis=1), "exp")
    scaling = lax.rsqrt(squares / (head_count * head_dim * n_exp) + eps_norm)
    normed_mix = (gated_out * scaling[:, None] * norm_gain[None, :]).astype(jnp.bfloat16)
    partial_value = jnp.dot(
        normed_mix,
        lax.all_gather(out_proj, "ctx", axis=1, tiled=True),
        preferred_element_type=jnp.float32,
    )
    gate_rows = w_gate[0]
    up_rows = w_up[0]
    down_rows = w_down[0]
    piece_width = gate_rows.shape[1]
    first_row = lax.axis_index("exp") * tok_quarter
    own_ids = lax.dynamic_slice_in_dim(route_ids, first_row, tok_quarter, 0)
    own_gates = lax.dynamic_slice_in_dim(route_gates, first_row, tok_quarter, 0)
    mixed_all = lax.psum(partial_value.astype(jnp.bfloat16), "exp").astype(jnp.float32)
    hidden_all = residual.astype(jnp.float32) + mixed_all
    moe_all = rms_rows(hidden_all, moe_gain)

    def place_quarter(quarter_rows, quarter_ids):
        return place_rows(quarter_rows, quarter_ids, experts, capacity)

    placed = jax.vmap(place_quarter)(
        moe_all.reshape(n_exp, tok_quarter, model_width),
        route_ids.reshape(n_exp, tok_quarter, route_ids.shape[1]),
    )
    placed = placed.reshape(n_exp * capacity, experts, model_width)
    outgoing = jnp.repeat(placed, PAIR, axis=1)
    arrived = lax.all_to_all(outgoing, "ctx", split_axis=1, concat_axis=1, tiled=True)
    flattened = arrived.reshape(-1, model_width)
    gate_val = jnp.dot(flattened, gate_rows, preferred_element_type=jnp.float32)
    up_val = jnp.dot(flattened, up_rows, preferred_element_type=jnp.float32)
    activated = (jax.nn.silu(gate_val) * up_val).astype(jnp.bfloat16)
    hidden = activated.reshape(arrived.shape[0], arrived.shape[1], piece_width)
    hidden_own = lax.dynamic_slice_in_dim(hidden_all, first_row, tok_quarter, 0)
    product = jnp.dot(
        hidden.reshape(-1, piece_width), down_rows, preferred_element_type=jnp.float32
    )
    rounded = lax.optimization_barrier(product.astype(jnp.bfloat16)).astype(jnp.float32)
    summed = lax.psum_scatter(
        rounded.reshape(lax.axis_size("exp") * capacity, hidden.shape[1], model_width).astype(
            jnp.bfloat16
        ),
        "exp",
        scatter_dimension=0,
        tiled=True,
    )
    halves = lax.all_to_all(summed, "ctx", split_axis=1, concat_axis=1, tiled=True)
    flattened, rank_ids = route_ranks(own_ids, experts)
    base_rows = rank_ids * n_ctx + flattened * PAIR
    fetch_rows = base_rows[:, None] + jnp.arange(PAIR, dtype=jnp.int32)[None, :]
    fetched = halves.reshape(capacity * n_ctx, model_width)[fetch_rows]
    expert_out = jnp.sum(fetched.astype(jnp.float32), axis=1)
    weighted = expert_out * own_gates.reshape(-1)[:, None]
    moe_out = jnp.sum(weighted.reshape(tok_quarter, -1, model_width), axis=1)
    return (hidden_own + moe_out).astype(jnp.bfloat16)


def solution(mesh):
    in_specs = (
        P("ctx", "exp"),
        P("ctx", "exp"),
        P("ctx", None),
        P("ctx", None),
        P("exp", "ctx"),
        P("exp", "ctx"),
        P("exp"),
        P("exp", None, None),
        P("exp"),
        P("exp", "ctx"),
        P("ctx", None),
        P(),
        P("ctx", None, "exp"),
        P("ctx", None, "exp"),
        P("ctx", "exp", None),
        P("ctx", None),
        P("ctx", None),
    )
    out_specs = P(("ctx", "exp"), None)
    return jax.shard_map(local, mesh=mesh, in_specs=in_specs, out_specs=out_specs, check_vma=False)
```

profile of v0, /device:TPU:1, one launch (start us, length us, event | category | flops | bytes accessed | tf_op | source)
XLA Modules:
  0.0 688.3 jit_solution(15999288479080339872)
XLA Ops:
  6.5 1.0 reduce_window_sum.33
  7.5 0.2 slice_reduce_fusion
  7.7 0.8 exponential_bitcast_fusion
  8.5 1.1 copy.109
  9.6 0.4 fusion.11
  10.0 0.1 broadcast_in_dim.29
  10.2 0.7 copy.110
  11.0 0.7 all-gather.5.cloned.1.call-update
  11.8 0.9 fusion.42
  12.6 55.4 %all-gather.3.cloned.1.call-done = bf16[32,16,65,128]{3,1,2,0:T(8,128)(2,1)} async-done(((bf16[1,16,65,128]{3,1,2,0:T(8,128)(2,1)}), bf16[32,16,65,128]{3,1,2,0:T(8,128)(2,1)}) %all-gather.3.cloned.1.call-update) | async-done | bytes 8519696 | tf_op jit(solution)/shard_map/all_gather | solution.py:17
  68.1 2.4 broadcast_in_dim.28
  70.5 7.9 %while.12 = (s32[]{:T(128)}, f32[16]{0:T(128)S(1)}, f32[16,64,128]{0,2,1:T(8,128)}, s32[]{:T(128)}, bf16[32,16,65,128]{3,1,2,0:T(8,128)(2,1)}, /*index=5*/s32[]{:T(128)}, s32[]{:T(128)}, s32[]{:T(128)}) while((s32[]{:T(128)}, f32[16]{0:T(128)S(1)}, f32[16,64,128]{0,2,1:T(8,128)}, s32[]{:T(128)}, bf16[32,16,65,128]{3,1,2,0:T(8,128)(2,1)}, ...), condition=%wide.region_2.3_spmd, body=%wide.region_1.2_spmd.sunk | while | flops 395285 | bytes 3437051 | solution.py:24
  70.5 1.0 constant_dynamic-slice_fusion.4
  71.5 1.4 copy.132
  72.9 0.5 bitcast_convert_fusion.2
  73.4 5.0 slice_add_fusion.2
  78.5 3.1 copy.112
  81.6 0.5 fusion.10
  82.1 1.4 fusion.9
  83.5 0.2 copy.115
  83.7 0.2 multiply_reduce_fusion.2
  83.9 8.4 %psum.14 = f32[128]{0:T(128)S(1)} all-reduce(f32[128]{0:T(128)S(1)} %multiply_reduce_fusion.2), channel_id=1, replica_groups=mesh['ctx'=32,'exp'=4] {'exp'}, use_global_device_ids=true, to_apply=%region_4.5 | all-reduce | flops 128 | bytes 1024 | tf_op jit(solution)/shard_map/psum | solution.py:113
  92.3 37.1 %all-gather.5.cloned.1.call-done = bf16[1024,4096]{1,0:T(8,128)(2,1)} async-done(((bf16[1024,128]{1,0:T(8,128)(2,1)}), bf16[1024,4096]{1,0:T(8,128)(2,1)}) %all-gather.5.cloned.1.call-update) | async-done | bytes 8388624 | tf_op jit(solution)/shard_map/all_gather | solution.py:118
  129.5 5.8 convolution_convert_fusion.2
  135.3 0.3 reduce-scatter.4.cloned.1.call-start
  135.6 0.1 copy.116
  135.7 0.1 eq.44
  135.9 0.1 fusion.35
  136.0 0.1 reduce_window_sum.34
  136.1 0.2 select_reduce_fusion
  136.3 240.4 %all-reduce.2.cloned.1.call-done = bf16[128,4096]{1,0:T(8,128)(2,1)} async-done(((bf16[128,4096]{1,0:T(8,128)(2,1)}), bf16[128,4096]{1,0:T(8,128)(2,1)}) %all-reduce.2.cloned.1.call-update) | async-done | bytes 1048592 | tf_op jit(solution)/shard_map/psum | solution.py:128
  376.8 3.0 convert_add_fusion
  379.8 0.4 multiply_convert_fusion.1
  380.2 3.4 broadcast_in_dim.30
  383.6 2.7 reshape.163
  386.4 1.4 convolution_convert_fusion.1
  387.8 2.3 copy.117
  390.1 4.3 broadcast_in_dim.31
  394.3 105.3 %all_to_all.10 = bf16[32,32,4096]{2,0,1:T(8,128)(2,1)} all-to-all(bf16[32,32,4096]{2,0,1:T(8,128)(2,1)} %bitcast.70), channel_id=1, replica_groups=mesh['ctx'=32,'exp'=4] {'ctx'}, dimensions={1} | all-to-all | bytes 16777216 | tf_op jit(solution)/shard_map/all_to_all | solution.py:141
  499.6 11.3 %copy.118 = bf16[32,32,4096]{2,1,0:T(8,128)(2,1)} copy(bf16[32,32,4096]{2,0,1:T(8,128)(2,1)} %all_to_all.10) | data formatting | bytes 16777216 | tf_op jit(solution)/shard_map/all_to_all | solution.py:141
  511.0 12.7 %fusion.2 = f32[1024,896]{1,0:T(8,128)S(1)} fusion(bf16[1024,4096]{1,0:T(8,128)(2,1)} %bitcast.72, bf16[1,4096,896]{2,1,0:T(8,128)(2,1)} %param.32), kind=kOutput, calls=%fused_computation.8 | convolution fusion | flops 7516192768 | bytes 19398656 | tf_op jit(solution)/shard_map/dot_general | solution.py:144
  523.7 9.2 %multiply_convert_fusion = bf16[1024,896]{1,0:T(8,128)(2,1)S(1)} fusion(f32[1024,896]{1,0:T(8,128)S(1)} %fusion.2, bf16[1024,4096]{1,0:T(8,128)(2,1)S(1)} %bitcast.73, bf16[1,4096,896]{2,1,0:T(8,128)(2,1)S(1)} %bitcast.81), kind=kOutput, calls=%fused_computation.14 | convolution fusion | flops 7521697792 | bytes 21233664 | tf_op jit(solution)/shard_map/dot_general | solution.py:143
  532.9 11.3 %convolution_convert_fusion = bf16[1024,4096]{1,0:T(8,128)(2,1)} fusion(bf16[1024,896]{1,0:T(8,128)(2,1)S(1)} %multiply_convert_fusion, bf16[1,896,4096]{2,1,0:T(8,128)(2,1)S(1)} %bitcast.83), kind=kOutput, calls=%fused_computation.6 | convolution fusion | flops 7520387072 | bytes 17563648 | tf_op jit(solution)/shard_map/dot_general | solution.py:148
  544.1 11.3 %copy.130 = bf16[4,8,32,4096]{3,1,2,0:T(8,128)(2,1)} copy(bf16[4,8,32,4096]{3,2,1,0:T(8,128)(2,1)} %bitcast.74) | data formatting | bytes 16777216
  555.5 77.8 %reduce-scatter.4.cloned.1.call-done = bf16[8,131072]{1,0:T(8,128)(2,1)} async-done(((bf16[32,131072]{1,0:T(8,128)(2,1)}), bf16[8,131072]{1,0:T(8,128)(2,1)}) %reduce-scatter.4.cloned.1.call-update) | async-done | bytes 2097168
  633.2 8.1 %all-to-all-start.1 = ((bf16[8,32,4096]{2,0,1:T(8,128)(2,1)}), bf16[8,32,4096]{2,0,1:T(8,128)(2,1)}, u32[]{:S(2)}, u32[]{:S(2)}) async-start(bf16[8,32,4096]{2,0,1:T(8,128)(2,1)} %bitcast.76), calls=%async_computation.1 | async-start | bytes 4194304 | tf_op jit(solution)/shard_map/all_to_all | solution.py:160
  641.4 0.1 constant_dynamic-slice_fusion.1
  641.5 0.1 copy.121
  641.5 0.1 eq.50
  641.7 0.1 fusion.39
  641.7 0.1 reduce_window_sum.35
  641.8 0.2 select_reduce_fusion.1
  642.0 0.1 compare_select_fusion
  642.1 0.1 reshape.171
  642.3 0.1 constant_dynamic-slice_fusion.2
  642.3 0.1 copy.122
  642.4 27.1 %all-to-all-done.1 = bf16[8,32,4096]{2,0,1:T(8,128)(2,1)} async-done(((bf16[8,32,4096]{2,0,1:T(8,128)(2,1)}), bf16[8,32,4096]{2,0,1:T(8,128)(2,1)}, u32[]{:S(2)}, u32[]{:S(2)}) %all-to-all-start.1) | async-done | bytes 2097184 | tf_op jit(solution)/shard_map/all_to_all | solution.py:160
  669.5 2.7 copy.120
  672.3 1.2 gather_fusion
  673.5 1.3 reshape.178
  674.8 2.7 reduce_sum.60
  677.5 0.6 reduce_sum.61
  678.2 1.4 multiply_reduce_fusion.1
  679.6 1.8 add_convert_fusion
  (55 shorter events, 0.3 us)
Async XLA Ops:
  6.5 3.1 copy-start
  6.5 61.5 %all-gather.3.cloned.1.call-start = ((), (), s32[]{:S(2)}) async-start(), calls=%async_computation.3 | async-start | bytes 8785920 | tf_op jit(solution)/shard_map/all_gather | solution.py:17
  10.9 118.5 %all-gather.5.cloned.1.call-start = ((), (), s32[]{:S(2)}) async-start(), calls=%async_computation.4 | async-start | bytes 8650752 | tf_op jit(solution)/shard_map/all_gather | solution.py:118
  11.7 365.1 %all-reduce.2.cloned.1.call-start = ((), (), s32[]{:S(2)}) async-start(), calls=%async_computation.5 | async-start | bytes 2097152 | tf_op jit(solution)/shard_map/psum | solution.py:128
  78.4 3.1 copy-start.5
  78.4 3.1 copy-start.7
  78.4 3.6 copy-start.9
  78.4 3.6 copy-start.13
  78.5 5.2 copy-start.6
  81.5 47.9 %copy-start.12 = (f32[1024]{0:T(1024)S(1)}, f32[1024]{0:T(1024)}, u32[]{:S(2)}) copy-start(f32[1024]{0:T(1024)} %param.27) | copy-start | bytes 12292
  92.3 43.3 %copy-start.10 = (s32[128,2]{0,1:T(2,128)S(1)}, s32[128,2]{0,1:T(2,128)}, u32[]{:S(2)}) copy-start(s32[128,2]{0,1:T(2,128)} %param.34) | copy-start | bytes 3076
  92.3 284.4 %copy-start.3 = (bf16[128,4096]{1,0:T(8,128)(2,1)S(1)}, bf16[128,4096]{1,0:T(8,128)(2,1)}, u32[]{:S(2)}) copy-start(bf16[128,4096]{1,0:T(8,128)(2,1)} %param.29) | copy-start | bytes 3145732
  135.3 244.5 %copy-start.8 = (f32[4096]{0:T(1024)S(1)}, f32[4096]{0:T(1024)}, u32[]{:S(2)}) copy-start(f32[4096]{0:T(1024)} %param.30) | copy-start | bytes 49156
  135.3 498.0 %reduce-scatter.4.cloned.1.call-start = ((), (), s32[]{:S(2)}) async-start(), calls=%async_computation.6 | async-start | bytes 10485760
  376.8 3.0 copy-start.4
  499.6 24.0 %slice-start = ((s8[7340032]{0:T(1024)(128)(4,1)}), s8[3145728]{0:T(1024)(128)(4,1)S(1)}, s32[]{:S(2)}) async-start(s8[7340032]{0:T(1024)(128)(4,1)} %bitcast.80), calls=%async_computation.7 | async-start | bytes 6291456
  511.0 12.7 %copy-start.2 = (bf16[32,32,4096]{2,1,0:T(8,128)(2,1)S(1)}, bf16[32,32,4096]{2,1,0:T(8,128)(2,1)}, u32[]{:S(2)}) copy-start(bf16[32,32,4096]{2,1,0:T(8,128)(2,1)} %copy.118) | copy-start | bytes 25165828
  511.0 12.7 %slice-start.1 = ((s8[7340032]{0:T(1024)(128)(4,1)}), s8[4194304]{0:T(1024)(128)(4,1)S(1)}, s32[]{:S(2)}) async-start(s8[7340032]{0:T(1024)(128)(4,1)} %bitcast.80), calls=%async_computation.8 | async-start | bytes 8388608
  511.0 21.9 %slice-start.2 = ((s8[7340032]{0:T(1024)(128)(4,1)}), s8[4194304]{0:T(1024)(128)(4,1)S(1)}, s32[]{:S(2)}) async-start(s8[7340032]{0:T(1024)(128)(4,1)} %bitcast.82), calls=%async_computation.9 | async-start | bytes 8388608
  523.7 9.2 %slice-start.3 = ((s8[7340032]{0:T(1024)(128)(4,1)}), s8[3145728]{0:T(1024)(128)(4,1)S(1)}, s32[]{:S(2)}) async-start(s8[7340032]{0:T(1024)(128)(4,1)} %bitcast.82), calls=%async_computation.10 | async-start | bytes 6291456
  555.5 86.8 %copy-start.11 = (f32[128,2]{0,1:T(2,128)S(1)}, f32[128,2]{0,1:T(2,128)}, u32[]{:S(2)}) copy-start(f32[128,2]{0,1:T(2,128)} %param.35) | copy-start | bytes 3076
  633.2 36.3 %all-to-all-start.1 = ((bf16[8,32,4096]{2,0,1:T(8,128)(2,1)}), bf16[8,32,4096]{2,0,1:T(8,128)(2,1)}, u32[]{:S(2)}, u32[]{:S(2)}) async-start(bf16[8,32,4096]{2,0,1:T(8,128)(2,1)} %bitcast.76), calls=%async_computation.1 | async-start | bytes 4194304 | tf_op jit(solution)/shard_map/all_to_all | solution.py:160
  673.5 8.0 %copy-start.1 = (bf16[128,128]{1,0:T(8,128)(2,1)S(1)}, bf16[128,128]{1,0:T(8,128)(2,1)}, u32[]{:S(2)}) copy-start(bf16[128,128]{1,0:T(8,128)(2,1)} %param.21) | copy-start | bytes 98308
Sparse Core Ops, SparseCore 0:
  11.0 56.9 all-gather.2
  70.2 59.1 all-gather.4
  135.4 241.3 all-reduce.1
  555.6 77.6 reduce-scatter.3
where the time goes:
time: 696 us; the launch traced here: 688 us
  waiting for transfers between devices  439 us (63%)
  blocking collectives  114 us (16%)
  local copies, waits for them, and re-layouts  52.4 us (8%)
  matrix products  43.4 us (6%)
  other arithmetic  17.9 us (3%)
  between operations  13.8 us (2%)
  starting transfers between devices  8.55 us (1%)
    psum x1, waiting for transfers between devices, local(): lax.psum(partial_value.astype(jnp.bfloat16), 'exp').astype(jnp.float32)  240 us
    all_to_all x1, blocking collectives, local(): lax.all_to_all(outgoing, 'ctx', split_axis=1, concat_axis=1, tiled=True)  105 us
    unnamed x5, waiting for transfers between devices  78.5 us
    all_gather x1, waiting for transfers between devices, entering(): gathered = lax.all_gather(packed.astype(jnp.bfloat16), axis)  55.4 us
    all_gather x1, waiting for transfers between devices, local(): lax.all_gather(out_proj, 'ctx', axis=1, tiled=True)  37.1 us
    all_to_all x1, waiting for transfers between devices, local(): lax.all_to_all(summed, 'ctx', split_axis=1, concat_axis=1, tiled=True)  27.1 us
  transfers between devices with their start and end apart: 5, of which 5 were waited for; matrix products, arithmetic and copies ran while one was open for 3% of the time, Pallas kernels for 0%

commit v1 on v0

--- a/solution.py
+++ b/solution.py
@@ -2,6 +2,7 @@
 import jax.numpy as jnp
 from jax import lax
 from jax.sharding import PartitionSpec as P
+from jax.lax import all_to_all, axis_size
 
 PAIR = 2
 eps_norm = 1e-05
@@ -73,6 +74,13 @@
     route_ids,
     route_gates,
 ):
+
+    def map_sites(xx, link_axis, array_axis):
+        before = axis_size(link_axis)
+        res = jnp.stack([xx] * before)
+        block_last = all_to_all(res, link_axis, 0, 0)
+        return jnp.concatenate(block_last, axis=array_axis)
+
     tok_ctx = inputs.shape[0]
     head_count = step_size.shape[0]
     head_dim = inputs.shape[1] // head_count
@@ -114,9 +122,7 @@
     scaling = lax.rsqrt(squares / (head_count * head_dim * n_exp) + eps_norm)
     normed_mix = (gated_out * scaling[:, None] * norm_gain[None, :]).astype(jnp.bfloat16)
     partial_value = jnp.dot(
-        normed_mix,
-        lax.all_gather(out_proj, "ctx", axis=1, tiled=True),
-        preferred_element_type=jnp.float32,
+        normed_mix, map_sites(out_proj, "ctx", 1), preferred_element_type=jnp.float32
     )
     gate_rows = w_gate[0]
     up_rows = w_up[0]

time: 696 us -> 777 us (1.12)
  waiting for transfers between devices: 439 us -> 502 us
  starting transfers between devices: 8.55 us -> 18.6 us
    all_gather x1, waiting for transfers between devices: 55.4 us -> 114 us  [entering(): gathered = lax.all_gather(packed.astype(jnp.bfloat16), axis)]
    psum x1, waiting for transfers between devices: 240 us -> 283 us  [local(): lax.psum(partial_value.astype(jnp.bfloat16), 'exp').astype(jnp.float32)]
    all_gather x1 -> x0, waiting for transfers between devices: 37.1 us -> none  [local(): lax.all_gather(out_proj, 'ctx', axis=1, tiled=True)]
    all_to_all x0 -> x1, starting transfers between devices: none -> 9.79 us  [map_sites(): block_last = all_to_all(res, link_axis, 0, 0)]
    unnamed x5 -> x4, waiting for transfers between devices: 78.5 us -> 77.8 us
  transfers between devices with their start and end apart: 5 -> 5, of which waited for: 5 -> 4; matrix products, arithmetic and copies ran while one was open for 3% -> 3% of each run, Pallas kernels for 0% -> 0%
where the time goes in v1:
time: 777 us; the launch traced here: 768 us
  waiting for transfers between devices  502 us (65%)
  blocking collectives  113 us (15%)
  local copies, waits for them, and re-layouts  57.7 us (7%)
  matrix products  44.3 us (6%)
  starting transfers between devices  18.6 us (2%)
  other arithmetic  17.9 us (2%)
  between operations  14 us (2%)
    psum x1, waiting for transfers between devices, local(): lax.psum(partial_value.astype(jnp.bfloat16), 'exp').astype(jnp.float32)  283 us
    all_gather x1, waiting for transfers between devices, entering(): gathered = lax.all_gather(packed.astype(jnp.bfloat16), axis)  114 us
    all_to_all x1, blocking collectives, local(): lax.all_to_all(outgoing, 'ctx', split_axis=1, concat_axis=1, tiled=True)  105 us
    unnamed x4, waiting for transfers between devices  77.8 us
    all_to_all x1, waiting for transfers between devices, local(): lax.all_to_all(summed, 'ctx', split_axis=1, concat_axis=1, tiled=True)  27.1 us
  transfers between devices with their start and end apart: 5, of which 4 were waited for; matrix products, arithmetic and copies ran while one was open for 3% of the time, Pallas kernels for 0%

profile of v1, /device:TPU:1, one launch (start us, length us, event | category | flops | bytes accessed | tf_op | source)
XLA Modules:
  0.0 767.9 jit_solution(12291094136630959188)
XLA Ops:
  6.5 1.0 reduce_window_sum.33
  7.5 0.2 slice_reduce_fusion
  7.7 0.8 exponential_bitcast_fusion
  8.5 1.1 copy.115
  9.6 0.4 fusion.11
  10.0 0.1 broadcast_in_dim.29
  10.2 0.8 copy.116
  11.0 1.1 copy.122
  12.1 4.3 stack.2
  16.4 9.8 %all-to-all-start = ((bf16[32,1024,128]{1,2,0:T(8,128)(2,1)}), bf16[32,1024,128]{1,2,0:T(8,128)(2,1)}, u32[]{:S(2)}, u32[]{:S(2)}) async-start(bf16[32,1024,128]{1,2,0:T(8,128)(2,1)} %stack.2), calls=%async_computation | async-start | bytes 16777216 | tf_op jit(solution)/shard_map/all_to_all | solution.py:81
  26.2 0.1 fusion.42
  26.4 114.2 %all-gather.2.cloned.1.call-done = bf16[32,16,65,128]{3,1,2,0:T(8,128)(2,1)} async-done(((bf16[1,16,65,128]{3,1,2,0:T(8,128)(2,1)}), bf16[32,16,65,128]{3,1,2,0:T(8,128)(2,1)}) %all-gather.2.cloned.1.call-update) | async-done | bytes 8519696 | tf_op jit(solution)/shard_map/all_gather | solution.py:18
  140.5 2.5 broadcast_in_dim.28
  143.0 8.0 %while.12 = (s32[]{:T(128)}, f32[16]{0:T(128)S(1)}, f32[16,64,128]{0,2,1:T(8,128)}, s32[]{:T(128)}, bf16[32,16,65,128]{3,1,2,0:T(8,128)(2,1)}, /*index=5*/s32[]{:T(128)}, s32[]{:T(128)}, s32[]{:T(128)}) while((s32[]{:T(128)}, f32[16]{0:T(128)S(1)}, f32[16,64,128]{0,2,1:T(8,128)}, s32[]{:T(128)}, bf16[32,16,65,128]{3,1,2,0:T(8,128)(2,1)}, ...), condition=%wide.region_2.3_spmd, body=%wide.region_1.2_spmd.sunk | while | flops 395285 | bytes 3437051 | solution.py:25
  143.0 1.0 constant_dynamic-slice_fusion.4
  144.0 1.4 copy.139
  145.4 0.5 bitcast_convert_fusion.2
  146.0 5.0 slice_add_fusion.2
  151.0 2.9 copy.118
  154.0 0.5 fusion.10
  154.4 1.4 fusion.9
  155.9 0.2 copy.121
  156.1 0.2 multiply_reduce_fusion.2
  156.3 8.4 %psum.14 = f32[128]{0:T(128)S(1)} all-reduce(f32[128]{0:T(128)S(1)} %multiply_reduce_fusion.2), channel_id=1, replica_groups=mesh['ctx'=32,'exp'=4] {'exp'}, use_global_device_ids=true, to_apply=%region_4.5 | all-reduce | flops 128 | bytes 1024 | tf_op jit(solution)/shard_map/psum | solution.py:121
  164.8 7.4 convolution_convert_fusion.2
  172.3 0.6 reduce-scatter.4.cloned.1.call-start
  172.8 0.1 copy.123
  173.0 0.1 eq.44
  173.1 0.1 fusion.35
  173.2 0.1 reduce_window_sum.34
  173.3 0.2 select_reduce_fusion
  173.5 282.8 %all-reduce.2.cloned.1.call-done = bf16[128,4096]{1,0:T(8,128)(2,1)} async-done(((bf16[128,4096]{1,0:T(8,128)(2,1)}), bf16[128,4096]{1,0:T(8,128)(2,1)}) %all-reduce.2.cloned.1.call-update) | async-done | bytes 1048592 | tf_op jit(solution)/shard_map/psum | solution.py:134
  456.4 3.0 convert_add_fusion
  459.4 0.4 multiply_convert_fusion.1
  459.8 3.4 broadcast_in_dim.30
  463.3 2.7 reshape.173
  466.0 1.4 convolution_convert_fusion.1
  467.4 2.3 copy.124
  469.7 4.3 broadcast_in_dim.31
  473.9 104.9 %all_to_all.15 = bf16[32,32,4096]{2,0,1:T(8,128)(2,1)} all-to-all(bf16[32,32,4096]{2,0,1:T(8,128)(2,1)} %bitcast.73), channel_id=1, replica_groups=mesh['ctx'=32,'exp'=4] {'ctx'}, dimensions={1} | all-to-all | bytes 16777216 | tf_op jit(solution)/shard_map/all_to_all | solution.py:147
  578.9 11.3 %copy.125 = bf16[32,32,4096]{2,1,0:T(8,128)(2,1)} copy(bf16[32,32,4096]{2,0,1:T(8,128)(2,1)} %all_to_all.15) | data formatting | bytes 16777216 | tf_op jit(solution)/shard_map/all_to_all | solution.py:147
  590.2 12.7 %fusion.2 = f32[1024,896]{1,0:T(8,128)S(1)} fusion(bf16[1024,4096]{1,0:T(8,128)(2,1)} %bitcast.75, bf16[1,4096,896]{2,1,0:T(8,128)(2,1)} %param.32), kind=kOutput, calls=%fused_computation.8 | convolution fusion | flops 7516192768 | bytes 19398656 | tf_op jit(solution)/shard_map/dot_general | solution.py:150
  603.0 9.2 %multiply_convert_fusion = bf16[1024,896]{1,0:T(8,128)(2,1)S(1)} fusion(f32[1024,896]{1,0:T(8,128)S(1)} %fusion.2, bf16[1024,4096]{1,0:T(8,128)(2,1)S(1)} %bitcast.76, bf16[1,4096,896]{2,1,0:T(8,128)(2,1)S(1)} %bitcast.84), kind=kOutput, calls=%fused_computation.14 | convolution fusion | flops 7521697792 | bytes 21233664 | tf_op jit(solution)/shard_map/dot_general | solution.py:149
  612.2 11.3 %convolution_convert_fusion = bf16[1024,4096]{1,0:T(8,128)(2,1)} fusion(bf16[1024,896]{1,0:T(8,128)(2,1)S(1)} %multiply_convert_fusion, bf16[1,896,4096]{2,1,0:T(8,128)(2,1)S(1)} %bitcast.86), kind=kOutput, calls=%fused_computation.6 | convolution fusion | flops 7520387072 | bytes 17563648 | tf_op jit(solution)/shard_map/dot_general | solution.py:154
  623.5 11.3 %copy.137 = bf16[4,8,32,4096]{3,1,2,0:T(8,128)(2,1)} copy(bf16[4,8,32,4096]{3,2,1,0:T(8,128)(2,1)} %bitcast.77) | data formatting | bytes 16777216
  634.8 77.8 %reduce-scatter.4.cloned.1.call-done = bf16[8,131072]{1,0:T(8,128)(2,1)} async-done(((bf16[32,131072]{1,0:T(8,128)(2,1)}), bf16[8,131072]{1,0:T(8,128)(2,1)}) %reduce-scatter.4.cloned.1.call-update) | async-done | bytes 2097168
  712.6 8.2 %all-to-all-start.2 = ((bf16[8,32,4096]{2,0,1:T(8,128)(2,1)}), bf16[8,32,4096]{2,0,1:T(8,128)(2,1)}, u32[]{:S(2)}, u32[]{:S(2)}) async-start(bf16[8,32,4096]{2,0,1:T(8,128)(2,1)} %bitcast.79), calls=%async_computation.2 | async-start | bytes 4194304 | tf_op jit(solution)/shard_map/all_to_all | solution.py:166
  720.8 0.1 constant_dynamic-slice_fusion.1
  720.9 0.1 copy.128
  720.9 0.1 eq.50
  721.1 0.1 reduce_window_sum.35
  721.2 0.2 select_reduce_fusion.1
  721.4 0.1 compare_select_fusion
  721.5 0.1 reshape.181
  721.7 0.1 constant_dynamic-slice_fusion.2
  721.7 0.1 copy.129
  721.8 27.1 %all-to-all-done.2 = bf16[8,32,4096]{2,0,1:T(8,128)(2,1)} async-done(((bf16[8,32,4096]{2,0,1:T(8,128)(2,1)}), bf16[8,32,4096]{2,0,1:T(8,128)(2,1)}, u32[]{:S(2)}, u32[]{:S(2)}) %all-to-all-start.2) | async-done | bytes 2097184 | tf_op jit(solution)/shard_map/all_to_all | solution.py:166
  748.9 2.7 copy.127
  751.7 1.2 gather_fusion
  752.9 1.3 reshape.188
  754.2 2.7 reduce_sum.60
  756.9 0.6 reduce_sum.61
  757.6 1.4 multiply_reduce_fusion.1
  759.0 1.8 add_convert_fusion
  (56 shorter events, 0.4 us)
Async XLA Ops:
  6.5 3.1 copy-start
  6.5 134.0 %all-gather.2.cloned.1.call-start = ((), (), s32[]{:S(2)}) async-start(), calls=%async_computation.4 | async-start | bytes 8785920 | tf_op jit(solution)/shard_map/all_gather | solution.py:18
  16.4 9.9 %copy-start.7 = (bf16[128,128]{1,0:T(8,128)(2,1)S(1)}, bf16[128,128]{1,0:T(8,128)(2,1)}, u32[]{:S(2)}) copy-start(bf16[128,128]{1,0:T(8,128)(2,1)} %param.22) | copy-start | bytes 98308
  16.4 148.4 %all-to-all-start = ((bf16[32,1024,128]{1,2,0:T(8,128)(2,1)}), bf16[32,1024,128]{1,2,0:T(8,128)(2,1)}, u32[]{:S(2)}, u32[]{:S(2)}) async-start(bf16[32,1024,128]{1,2,0:T(8,128)(2,1)} %stack.2), calls=%async_computation | async-start | bytes 16777216 | tf_op jit(solution)/shard_map/all_to_all | solution.py:81
  26.2 430.2 %all-reduce.2.cloned.1.call-start = ((), (), s32[]{:S(2)}) async-start(), calls=%async_computation.5 | async-start | bytes 2097152 | tf_op jit(solution)/shard_map/psum | solution.py:134
  151.0 3.0 copy-start.5
  151.0 3.4 copy-start.9
  151.0 3.5 copy-start.13
  151.0 5.1 copy-start.6
  153.9 10.8 %copy-start.12 = (f32[1024]{0:T(1024)S(1)}, f32[1024]{0:T(1024)}, u32[]{:S(2)}) copy-start(f32[1024]{0:T(1024)} %param.27) | copy-start | bytes 12292
  164.8 8.1 %copy-start.10 = (s32[128,2]{0,1:T(2,128)S(1)}, s32[128,2]{0,1:T(2,128)}, u32[]{:S(2)}) copy-start(s32[128,2]{0,1:T(2,128)} %param.34) | copy-start | bytes 3076
  164.8 291.6 %copy-start.3 = (bf16[128,4096]{1,0:T(8,128)(2,1)S(1)}, bf16[128,4096]{1,0:T(8,128)(2,1)}, u32[]{:S(2)}) copy-start(bf16[128,4096]{1,0:T(8,128)(2,1)} %param.29) | copy-start | bytes 3145732
  172.2 287.2 %copy-start.8 = (f32[4096]{0:T(1024)S(1)}, f32[4096]{0:T(1024)}, u32[]{:S(2)}) copy-start(f32[4096]{0:T(1024)} %param.30) | copy-start | bytes 49156
  172.3 540.3 %reduce-scatter.4.cloned.1.call-start = ((), (), s32[]{:S(2)}) async-start(), calls=%async_computation.6 | async-start | bytes 10485760
  456.4 3.0 copy-start.4
  578.9 24.0 %slice-start = ((s8[7340032]{0:T(1024)(128)(4,1)}), s8[3145728]{0:T(1024)(128)(4,1)S(1)}, s32[]{:S(2)}) async-start(s8[7340032]{0:T(1024)(128)(4,1)} %bitcast.83), calls=%async_computation.7 | async-start | bytes 6291456
  590.2 12.7 %copy-start.2 = (bf16[32,32,4096]{2,1,0:T(8,128)(2,1)S(1)}, bf16[32,32,4096]{2,1,0:T(8,128)(2,1)}, u32[]{:S(2)}) copy-start(bf16[32,32,4096]{2,1,0:T(8,128)(2,1)} %copy.125) | copy-start | bytes 25165828
  590.2 12.7 %slice-start.1 = ((s8[7340032]{0:T(1024)(128)(4,1)}), s8[4194304]{0:T(1024)(128)(4,1)S(1)}, s32[]{:S(2)}) async-start(s8[7340032]{0:T(1024)(128)(4,1)} %bitcast.83), calls=%async_computation.8 | async-start | bytes 8388608
  590.2 21.9 %slice-start.2 = ((s8[7340032]{0:T(1024)(128)(4,1)}), s8[4194304]{0:T(1024)(128)(4,1)S(1)}, s32[]{:S(2)}) async-start(s8[7340032]{0:T(1024)(128)(4,1)} %bitcast.85), calls=%async_computation.9 | async-start | bytes 8388608
  603.0 9.2 %slice-start.3 = ((s8[7340032]{0:T(1024)(128)(4,1)}), s8[3145728]{0:T(1024)(128)(4,1)S(1)}, s32[]{:S(2)}) async-start(s8[7340032]{0:T(1024)(128)(4,1)} %bitcast.85), calls=%async_computation.10 | async-start | bytes 6291456
  634.8 86.8 %copy-start.11 = (f32[128,2]{0,1:T(2,128)S(1)}, f32[128,2]{0,1:T(2,128)}, u32[]{:S(2)}) copy-start(f32[128,2]{0,1:T(2,128)} %param.35) | copy-start | bytes 3076
  712.6 36.3 %all-to-all-start.2 = ((bf16[8,32,4096]{2,0,1:T(8,128)(2,1)}), bf16[8,32,4096]{2,0,1:T(8,128)(2,1)}, u32[]{:S(2)}, u32[]{:S(2)}) async-start(bf16[8,32,4096]{2,0,1:T(8,128)(2,1)} %bitcast.79), calls=%async_computation.2 | async-start | bytes 4194304 | tf_op jit(solution)/shard_map/all_to_all | solution.py:166
  752.9 8.0 %copy-start.1 = (bf16[128,128]{1,0:T(8,128)(2,1)S(1)}, bf16[128,128]{1,0:T(8,128)(2,1)}, u32[]{:S(2)}) copy-start(bf16[128,128]{1,0:T(8,128)(2,1)} %param.21) | copy-start | bytes 98308
Sparse Core Ops, SparseCore 0:
  11.1 129.4 all-gather.1
  172.4 283.9 all-reduce.1
  634.9 77.6 reduce-scatter.3
